TPU v7x, 32 devices: a whole 2x2x4 slice. The times are simulated.
32 devices in a mesh: row: 2 (over y), col: 4 (over x, core), frame: 4 (over z).
Axes of the slice: x: 2, y: 2, z: 4, core: 2. Of those that a mesh axis runs over, the one named last changes fastest.
Arguments:
- video: float32 [16, 576, 1024], P('frame', 'row', 'col'), may hold values from -60 to 60
- multiplier: float32 [16, 576, 1024], P('frame', 'row', 'col'), may hold values from -3 to 3
- foreground: float32 [16, 576, 1024], P('frame', 'row', 'col'), may hold values from -6 to 6
- basis: float32 [16, 576, 1024], P(None, 'row', 'col'), may hold values from -40 to 40
- coefficients: float32 [16, 16], P('frame'), may hold values from -10 to 10
Outputs:
- new_foreground: float32 [16, 576, 1024], P('frame', 'row', 'col')
- new_coefficients: float32 [16, 16], P('frame')
- new_basis: float32 [16, 576, 1024], P(None, ('row', 'frame'), 'col')
All inputs are finite; a program needn't handle non-finite values.
Results may differ from a plain program's by a relative error of at most 0.0003.
Values sent between devices are 32-bit elements; how exact they have to be, the bound alone decides.
A program may use at most 128 MiB of HBM per device.

v0:
```python
import jax
import jax.numpy as jnp
from jax import lax
from jax.sharding import PartitionSpec as P

PASSES = 3


relax_rate = 0.8
smooth_weight = 0.5
smooth_floor = 0.25
shrink_level = 0.4
dual_scale = 0.8
ridge_share = 0.1


def with_halo(block, sides, width):
    for axis, dim in sides:
        count = lax.axis_size(axis)
        forward = [(i, i + 1) for i in range(count - 1)]
        backward = [(target, source) for source, target in forward]
        low = lax.ppermute(
            lax.slice_in_dim(block, block.shape[dim] - width, None, axis=dim), axis, forward
        )
        high = lax.ppermute(lax.slice_in_dim(block, 0, width, axis=dim), axis, backward)
        block = jnp.concatenate([low, block, high], axis=dim)
    return block


def forward_cells(padded, direction, shape):
    starts = [0, 0, 0]
    starts[direction] = 1
    limits = [starts[axis_dim] + shape[axis_dim] for axis_dim in range(3)]
    return lax.slice(padded, starts, limits)


def descend(padded, source, anchor, extent):
    shape = tuple((int(length) - 1 for length in padded.shape))
    here_cells = padded[:-1, :-1, :-1]
    slopes = []
    for direction in range(3):
        ahead_cells = forward_cells(padded, direction, shape)
        places = anchor[direction] + jnp.arange(shape[direction], dtype=jnp.int32)
        inside = (places >= 0) & (places < extent[direction] - 1)
        layout = [1, 1, 1]
        layout[direction] = shape[direction]
        inside = inside.reshape(layout)
        slopes.append(jnp.where(inside, ahead_cells - here_cells, jnp.zeros_like(here_cells)))
    weight = lax.rsqrt(
        smooth_floor + slopes[0] * slopes[0] + slopes[1] * slopes[1] + slopes[2] * slopes[2]
    )
    fluxes = [slope_part * weight for slope_part in slopes]
    spread = (
        fluxes[0][1:, 1:, 1:]
        - fluxes[0][:-1, 1:, 1:]
        + (fluxes[1][1:, 1:, 1:] - fluxes[1][1:, :-1, 1:])
        + (fluxes[2][1:, 1:, 1:] - fluxes[2][1:, 1:, :-1])
    )
    center = padded[1:-1, 1:-1, 1:-1]
    return center + relax_rate * (source - center + smooth_weight * spread)


def solve_definite(matrix, right_side):
    factor_lower = jnp.linalg.cholesky(matrix)
    half_solved = lax.linalg.triangular_solve(factor_lower, right_side, left_side=True, lower=True)
    return lax.linalg.triangular_solve(
        factor_lower, half_solved, left_side=True, lower=True, transpose_a=True
    )


def local(video, multiplier, foreground, basis, coefficients):
    highest = lax.Precision.HIGHEST
    frames_here, rows_here, cols_here = video.shape
    rank_size = basis.shape[0]
    frame_count = lax.axis_size("frame")
    row_count = lax.axis_size("row")
    col_count = lax.axis_size("col")
    extent = (frames_here * frame_count, rows_here * row_count, cols_here * col_count)
    frame_slot = lax.axis_index("frame")
    corner = (
        frame_slot * frames_here,
        lax.axis_index("row") * rows_here,
        lax.axis_index("col") * cols_here,
    )
    pixels = rows_here * cols_here
    flat_basis = basis.reshape(rank_size, pixels)
    background = jnp.dot(coefficients, flat_basis, precision=highest).reshape(video.shape)
    target = video - background + dual_scale * multiplier
    current = foreground
    for sweep in range(PASSES):
        padded = with_halo(current, (("row", 1), ("col", 2), ("frame", 0)), 1)
        current = descend(padded, target, tuple((start_cell - 1 for start_cell in corner)), extent)
    shrunk = current - jnp.clip(current, -shrink_level, shrink_level)
    residual_target = video + dual_scale * multiplier - shrunk
    flat_target = residual_target.reshape(frames_here, pixels)
    gram_part = jnp.dot(flat_basis, flat_basis.T, precision=highest)
    cross_part = jnp.dot(flat_basis, flat_target.T, precision=highest)
    gram_sum, cross_sum = lax.psum((gram_part, cross_part), ("row", "col"))
    identity_matrix = jnp.eye(rank_size, dtype=gram_sum.dtype)
    pixel_ridge = ridge_share * pixels * row_count * col_count
    coeff_rows = solve_definite(
        gram_sum + pixel_ridge * identity_matrix, cross_sum + pixel_ridge * coefficients.T
    )
    total_part = jnp.dot(coeff_rows, flat_target, precision=highest).reshape(
        rank_size, rows_here, cols_here
    )
    frame_gram_part = jnp.dot(coeff_rows, coeff_rows.T, precision=highest)
    owned_rows = rows_here // frame_count
    owned_sums = lax.psum_scatter(total_part, "frame", scatter_dimension=1, tiled=True)
    frame_gram = lax.psum(frame_gram_part, "frame")
    old_owned = lax.dynamic_slice_in_dim(basis, frame_slot * owned_rows, owned_rows, 1)
    frame_ridge = ridge_share * frames_here * frame_count
    right_side = (owned_sums + frame_ridge * old_owned).reshape(rank_size, owned_rows * cols_here)
    new_basis = solve_definite(frame_gram + frame_ridge * identity_matrix, right_side)
    return (shrunk, coeff_rows.T, new_basis.reshape(rank_size, owned_rows, cols_here))


def solution(mesh):
    placed = (
        P("frame", "row", "col"),
        P("frame", "row", "col"),
        P("frame", "row", "col"),
        P(None, "row", "col"),
        P("frame", None),
    )
    return jax.shard_map(
        local,
        mesh=mesh,
        in_specs=placed,
        out_specs=(P("frame", "row", "col"), P("frame", None), P(None, ("row", "frame"), "col")),
        check_vma=False,
    )
```

profile of v0, /device:TPU:0, one launch (start us, length us, event | category | flops | bytes accessed | tf_op | source)
XLA Modules:
  0.0 317.2 jit_solution(16759159674767453106)
XLA Ops:
  8.0 4.9 %collective-permute-start = (f32[4,1,256]{2,0,1:T(4,128)S(1)}, f32[4,1,256]{2,0,1:T(4,128)S(1)}, u32[]{:S(2)}, u32[]{:S(2)}) collective-permute-start(f32[4,1,256]{2,0,1:T(4,128)S(1)} %copy.117), channel_id=1, source_target_pairs={{0,16},{1,17},{2,18},{3,19},{4,20},{5,21},{6,22},{7,23},{8,24},{9,... | collective-permute-start | bytes 12296 | tf_op jit(solution)/shard_map/ppermute | solution.py:22
  14.2 2.1 constant_dynamic-update-slice_fusion.1
  16.3 2.1 collective-permute-done.1
  22.3 3.1 collective-permute-done.3
  25.8 3.2 %pad_maximum_fusion.27 = (f32[1,290,258]{2,0,1:T(1,128)S(1)}, f32[1,290,258]{2,0,1:T(1,128)S(1)}) fusion(f32[4,290,1]{2,0,1:T(4,128)S(1)} %copy.54, f32[4,290,256]{2,0,1:T(4,128)S(1)} %constant_dynamic-update-slice_fusion, f32[4,290,1]{2,0,1:T(4,128)S(1)} %copy.53), kind=kLoop, calls=%fused_computation.97 | loop fusion | flops 299280 | bytes 1795680 | tf_op jit(solution)/shard_map/slice | solution.py:25
  29.1 3.5 %collective-permute-start.5 = (f32[1,290,258]{2,0,1:T(1,128)S(1)}, f32[1,290,258]{2,0,1:T(1,128)S(1)}, u32[]{:S(2)}, u32[]{:S(2)}) collective-permute-start(f32[1,290,258]{2,0,1:T(1,128)S(1)} %get-tuple-element.32), channel_id=1, source_target_pairs={{0,1},{1,2},{2,3},{4,5},{5,6},{6,7},{8,9},{9,10},{10,11},{12,13},{... | collective-permute-start | bytes 897848 | tf_op jit(solution)/shard_map/ppermute | solution.py:22
  32.6 1.5 collective-permute-start.4
  34.2 7.6 %collective-permute-done.5 = f32[1,290,258]{2,0,1:T(1,128)S(1)} collective-permute-done((f32[1,290,258]{2,0,1:T(1,128)S(1)}, f32[1,290,258]{2,0,1:T(1,128)S(1)}, u32[]{:S(2)}, u32[]{:S(2)}) %collective-permute-start.5) | collective-permute-done | bytes 299312 | tf_op jit(solution)/shard_map/ppermute | solution.py:22
  41.7 1.5 maximum_maximum_fusion
  43.3 3.2 %collective-permute-done.4 = f32[1,290,258]{2,0,1:T(1,128)S(1)} collective-permute-done((f32[1,290,258]{2,0,1:T(1,128)S(1)}, f32[1,290,258]{2,0,1:T(1,128)S(1)}, u32[]{:S(2)}, u32[]{:S(2)}) %collective-permute-start.4) | collective-permute-done | bytes 299312 | tf_op jit(solution)/shard_map/ppermute | solution.py:25
  46.5 4.6 %fusion.78 = (f32[5,289,257]{2,0,1:T(8,128)}, f32[5,289,257]{2,0,1:T(8,128)S(1)}) fusion(f32[5,290,258]{2,0,1:T(8,128)S(1)} %maximum_maximum_fusion, f32[1,290,258]{2,0,1:T(1,128)S(1)} %collective-permute-done.4, f32[4,290,1]{2,0,1:T(4,128)S(1)} %copy.54, f32[4,290,256]{2,0,1:T(4,128)S(1)} %constant_dynamic-update-slice_fusion, f32[4,290,1]{2,0,1:T(4,128)S(1)} %copy.53, ...), kind=kLoop, calls=%fused_computation.146 | loop fusion | flops 5941840 | bytes 8924251 | tf_op jit(solution)/shard_map/mul | solution.py:52
  51.2 2.1 fusion.47
  53.4 12.9 %fusion.40 = (f32[4,288,256]{2,0,1:T(4,128)S(1)}, f32[4,288,256]{2,0,1:T(4,128)}) fusion(f32[5,289,257]{2,0,1:T(8,128)S(1)} %get-tuple-element.26, f32[5,289,257]{2,0,1:T(8,128)S(1)} %get-tuple-element.25, f32[5,289,257]{2,0,1:T(8,128)} %get-tuple-element.19, f32[4,288,256]{2,1,0:T(8,128)S(1)} %copy-done.7, f32[4,288,256]{2,1,0:T(8,128)S(1)} %copy-done, ...), kind=kOutput, calls=%fused_computation.71 | convolution fusion | flops 60456960 | bytes 17694976 | tf_op jit(solution)/shard_map/dot_general | solution.py:87
  66.3 2.5 collective-permute-start.6
  70.1 4.2 %collective-permute-done.7 = f32[4,1,256]{2,0,1:T(4,128)S(1)} collective-permute-done((f32[4,1,256]{2,0,1:T(4,128)S(1)}, f32[4,1,256]{2,0,1:T(4,128)S(1)}, u32[]{:S(2)}, u32[]{:S(2)}) %collective-permute-start.7) | collective-permute-done | bytes 4128 | tf_op jit(solution)/shard_map/ppermute | solution.py:25
  75.8 1.4 collective-permute-start.8
  77.5 1.7 collective-permute-start.9
  79.6 1.7 collective-permute-done.9
  82.3 5.3 %pad_maximum_fusion.24 = (f32[1,290,258]{2,0,1:T(1,128)S(1)}, f32[1,290,258]{2,0,1:T(1,128)S(1)}) fusion(f32[4,290,1]{2,0,1:T(4,128)S(1)} %copy.59, f32[4,290,1]{2,0,1:T(4,128)S(1)} %copy.58, f32[4,1,256]{2,0,1:T(4,128)S(1)} %collective-permute-done.7, f32[4,288,256]{2,0,1:T(4,128)S(1)} %get-tuple-element.45, f32[4,1,256]{2,0,1:T(4,128)S(1)} %collective-permute-done.6), kind=kLoop, calls=%fused_computation.94 | loop fusion | flops 598560 | bytes 1795680 | tf_op jit(solution)/shard_map/slice | solution.py:25
  87.6 3.5 %collective-permute-start.11 = (f32[1,290,258]{2,0,1:T(1,128)S(1)}, f32[1,290,258]{2,0,1:T(1,128)S(1)}, u32[]{:S(2)}, u32[]{:S(2)}) collective-permute-start(f32[1,290,258]{2,0,1:T(1,128)S(1)} %get-tuple-element.30), channel_id=1, source_target_pairs={{0,1},{1,2},{2,3},{4,5},{5,6},{6,7},{8,9},{9,10},{10,11},{12,13},{... | collective-permute-start | bytes 897848 | tf_op jit(solution)/shard_map/ppermute | solution.py:22
  92.4 7.9 %collective-permute-done.11 = f32[1,290,258]{2,0,1:T(1,128)S(1)} collective-permute-done((f32[1,290,258]{2,0,1:T(1,128)S(1)}, f32[1,290,258]{2,0,1:T(1,128)S(1)}, u32[]{:S(2)}, u32[]{:S(2)}) %collective-permute-start.11) | collective-permute-done | bytes 299312 | tf_op jit(solution)/shard_map/ppermute | solution.py:22
  100.3 1.5 maximum_maximum_fusion.1
  101.8 3.2 collective-permute-done.10
  105.0 4.5 %fusion.79 = (f32[5,289,257]{2,0,1:T(8,128)S(1)}, f32[5,289,257]{2,0,1:T(8,128)S(1)}) fusion(f32[5,290,258]{2,0,1:T(8,128)S(1)} %maximum_maximum_fusion.1, f32[1,290,258]{2,0,1:T(1,128)S(1)} %collective-permute-done.10, f32[4,290,1]{2,0,1:T(4,128)S(1)} %copy.59, f32[4,1,256]{2,0,1:T(4,128)S(1)} %collective-permute-done.7, ...), kind=kLoop, calls=%fused_computation.147 | loop fusion | flops 6684570 | bytes 8924251 | tf_op jit(solution)/shard_map/mul | solution.py:52
  109.5 2.1 fusion.48
  111.7 3.3 %fusion.34 = f32[4,288,256]{2,0,1:T(4,128)S(1)} fusion(f32[4,288,256]{2,0,1:T(4,128)S(1)} %get-tuple-element.45, f32[5,289,257]{2,0,1:T(8,128)S(1)} %get-tuple-element.24, f32[5,289,257]{2,0,1:T(8,128)S(1)} %get-tuple-element.23, f32[5,289,257]{2,0,1:T(8,128)S(1)} %get-tuple-element.17, f32[4,288,256]{2,0,1:T(4,128)S(1)} %copy-done.4), kind=kLoop, calls=%fused_computation.62 | loop fusion | flops 2949120 | bytes 10616832 | tf_op jit(solution)/shard_map/add | solution.py:60
  115.0 1.7 collective-permute-start.12
  117.9 4.2 %collective-permute-done.13 = f32[4,1,256]{2,0,1:T(4,128)S(1)} collective-permute-done((f32[4,1,256]{2,0,1:T(4,128)S(1)}, f32[4,1,256]{2,0,1:T(4,128)S(1)}, u32[]{:S(2)}, u32[]{:S(2)}) %collective-permute-start.13) | collective-permute-done | bytes 4128 | tf_op jit(solution)/shard_map/ppermute | solution.py:25
  128.3 2.4 collective-permute-done.15
  131.7 6.7 %pad_maximum_fusion.19 = (f32[1,290,258]{2,0,1:T(1,128)S(1)}, f32[1,290,258]{2,0,1:T(1,128)S(1)}) fusion(f32[4,290,1]{2,0,1:T(4,128)} %copy.63, f32[4,290,1]{2,0,1:T(4,128)S(1)} %copy.62, f32[4,1,256]{2,0,1:T(4,128)S(1)} %collective-permute-done.13, f32[4,288,256]{2,0,1:T(4,128)S(1)} %fusion.34, f32[4,1,256]{2,0,1:T(4,128)S(1)} %collective-permute-done.12), kind=kLoop, calls=%fused_computation.89 | loop fusion | flops 598560 | bytes 1795680 | tf_op jit(solution)/shard_map/slice | solution.py:25
  138.4 3.5 %collective-permute-start.17 = (f32[1,290,258]{2,0,1:T(1,128)S(1)}, f32[1,290,258]{2,0,1:T(1,128)S(1)}, u32[]{:S(2)}, u32[]{:S(2)}) collective-permute-start(f32[1,290,258]{2,0,1:T(1,128)S(1)} %get-tuple-element.28), channel_id=1, source_target_pairs={{0,1},{1,2},{2,3},{4,5},{5,6},{6,7},{8,9},{9,10},{10,11},{12,13},{... | collective-permute-start | bytes 897848 | tf_op jit(solution)/shard_map/ppermute | solution.py:22
  141.9 1.5 collective-permute-start.16
  143.4 14.2 %convolution_bitcast_fusion = f32[16,16]{1,0:T(8,128)S(1)} fusion(f32[16,288,256]{2,1,0:T(8,128)} %param.9), kind=kOutput, calls=%fused_computation.80 | convolution fusion | flops 226492416 | bytes 4719616 | tf_op jit(solution)/shard_map/dot_general | solution.py:96
  157.6 1.5 maximum_maximum_fusion.2
  159.2 4.8 %fusion.80 = (f32[5,289,257]{2,0,1:T(8,128)S(1)}, f32[5,289,257]{2,0,1:T(8,128)S(1)}) fusion(f32[5,290,258]{2,0,1:T(8,128)S(1)} %maximum_maximum_fusion.2, f32[1,290,258]{2,0,1:T(1,128)S(1)} %collective-permute-done.16, f32[4,290,1]{2,0,1:T(4,128)S(1)} %copy-done.6, f32[4,1,256]{2,0,1:T(4,128)S(1)} %collective-permute-done.13, ...), kind=kLoop, calls=%fused_computation.148 | loop fusion | flops 6684570 | bytes 8924251 | tf_op jit(solution)/shard_map/mul | solution.py:52
  164.0 2.2 fusion.49
  166.2 3.4 %clamp_subtract_fusion = f32[4,288,256]{2,0,1:T(4,128)S(1)} fusion(f32[4,288,256]{2,0,1:T(4,128)S(1)} %fusion.34, f32[5,289,257]{2,0,1:T(8,128)S(1)} %get-tuple-element.22, f32[5,289,257]{2,0,1:T(8,128)S(1)} %get-tuple-element.21, f32[5,289,257]{2,0,1:T(8,128)S(1)} %get-tuple-element.15, f32[4,288,256]{2,0,1:T(4,128)S(1)} %copy-done.5), kind=kLoop, calls=%fused_computation.40 | loop fusion | flops 3538944 | bytes 10616832 | tf_op jit(solution)/shard_map/sub | solution.py:93
  169.7 10.2 %convolution_bitcast_fusion.1 = f32[16,4]{0,1:T(4,128)} fusion(f32[16,288,256]{2,1,0:T(8,128)S(1)} %bitcast.90, f32[4,288,256]{2,0,1:T(4,128)S(1)} %clamp_subtract_fusion, f32[4,288,256]{2,1,0:T(8,128)S(1)} %copy-done.2, f32[4,288,256]{2,1,0:T(8,128)S(1)} %copy-done), kind=kOutput, calls=%fused_computation.81 | convolution fusion | flops 57507840 | bytes 8257792 | tf_op jit(solution)/shard_map/dot_general | solution.py:97
  179.9 24.6 %all-reduce = (f32[16,16]{1,0:T(8,128)S(1)}, f32[16,4]{0,1:T(4,128)}) all-reduce(f32[16,16]{1,0:T(8,128)S(1)} %convolution_bitcast_fusion, f32[16,4]{0,1:T(4,128)} %convolution_bitcast_fusion.1), channel_id=1, replica_groups=mesh['row'=2,'col'=4,'frame'=4] {'row','col'}, use_global_device_ids=true, to_apply=%region_0.1 | all-reduce | flops 320 | bytes 2560 | tf_op jit(solution)/shard_map/psum | solution.py:98
  207.3 1.4 cholesky.44
  210.7 1.9 custom-call.12
  213.6 6.6 %fusion.42 = f32[16,288,256]{2,0,1:T(8,128)} fusion(f32[16,4]{0,1:T(4,128)S(1)} %fusion.56, f32[4,288,256]{2,0,1:T(4,128)S(1)} %clamp_subtract_fusion, f32[4,288,256]{2,1,0:T(8,128)S(1)} %copy-done.3, f32[4,288,256]{2,1,0:T(8,128)S(1)} %copy-done), kind=kOutput, calls=%fused_computation.75 | convolution fusion | flops 57507840 | bytes 8257792 | tf_op jit(solution)/shard_map/dot_general | solution.py:104
  220.2 7.2 %copy.64 = f32[16,288,256]{2,0,1:T(8,128)} copy(f32[16,288,256]{2,1,0:T(8,128)} %param.9) | data formatting | bytes 9437184 | tf_op args[3]
  228.8 11.7 %psum.23 = f32[16,16]{1,0:T(8,128)S(1)} all-reduce(f32[16,16]{1,0:T(8,128)S(1)} %fusion.87), channel_id=1, replica_groups=mesh['row'=2,'col'=4,'frame'=4] {'frame'}, use_global_device_ids=true, to_apply=%region_4.6 | all-reduce | flops 256 | bytes 2048 | tf_op jit(solution)/shard_map/psum | solution.py:110
  240.7 1.5 cholesky.55
  244.7 59.6 %reduce-scatter.2.cloned.1.call-done = f32[16,72,256]{2,0,1:T(8,128)} async-done(((f32[16,288,256]{2,0,1:T(8,128)}), f32[16,72,256]{2,0,1:T(8,128)}) %reduce-scatter.2.cloned.1.call-update) | async-done | bytes 1179664 | tf_op jit(solution)/shard_map/reduce_scatter | solution.py:109
  304.3 2.8 fusion.21
  308.2 1.7 copy.77
  (113 shorter events, 31.6 us)
Async XLA Ops:
  7.2 297.1 %reduce-scatter.2.cloned.1.call-start = ((), (), s32[]{:S(2)}) async-start(), calls=%async_computation.1 | async-start | bytes 5898240 | tf_op jit(solution)/shard_map/reduce_scatter | solution.py:109
  8.0 6.2 %collective-permute-start = (f32[4,1,256]{2,0,1:T(4,128)S(1)}, f32[4,1,256]{2,0,1:T(4,128)S(1)}, u32[]{:S(2)}, u32[]{:S(2)}) collective-permute-start(f32[4,1,256]{2,0,1:T(4,128)S(1)} %copy.117), channel_id=1, source_target_pairs={{0,16},{1,17},{2,18},{3,19},{4,20},{5,21},{6,22},{7,23},{8,24},{9,... | collective-permute-start | bytes 12296 | tf_op jit(solution)/shard_map/ppermute | solution.py:22
  12.9 5.5 %collective-permute-start.1 = (f32[4,1,256]{2,0,1:T(4,128)S(1)}, f32[4,1,256]{2,0,1:T(4,128)S(1)}, u32[]{:S(2)}, u32[]{:S(2)}) collective-permute-start(f32[4,1,256]{2,0,1:T(4,128)S(1)} %copy.118), channel_id=1, source_target_pairs={{16,0},{17,1},{18,2},{19,3},{20,4},{21,5},{22,6},{23,7},{24,8},{25... | collective-permute-start | bytes 12296 | tf_op jit(solution)/shard_map/ppermute | solution.py:25
  19.1 2.9 collective-permute-start.2
  20.7 4.8 %collective-permute-start.3 = (f32[4,290,1]{1,0,2:T(4,128)S(1)}, f32[4,290,1]{1,0,2:T(4,128)S(1)}, u32[]{:S(2)}, u32[]{:S(2)}) collective-permute-start(f32[4,290,1]{1,0,2:T(4,128)S(1)} %copy.52), channel_id=1, source_target_pairs={{4,0},{8,4},{12,8},{5,1},{9,5},{13,9},{6,2},{10,6},{14,10},{7,3},{... | collective-permute-start | bytes 13928 | tf_op jit(solution)/shard_map/ppermute | solution.py:25
  29.1 12.7 %collective-permute-start.5 = (f32[1,290,258]{2,0,1:T(1,128)S(1)}, f32[1,290,258]{2,0,1:T(1,128)S(1)}, u32[]{:S(2)}, u32[]{:S(2)}) collective-permute-start(f32[1,290,258]{2,0,1:T(1,128)S(1)} %get-tuple-element.32), channel_id=1, source_target_pairs={{0,1},{1,2},{2,3},{4,5},{5,6},{6,7},{8,9},{9,10},{10,11},{12,13},{... | collective-permute-start | bytes 897848 | tf_op jit(solution)/shard_map/ppermute | solution.py:22
  32.6 18.5 %copy-start.9 = (pred[289]{0:T(512)(128)(4,1)}, pred[289]{0:T(512)(128)(4,1)S(1)}, u32[]{:S(2)}) copy-start(pred[289]{0:T(512)(128)(4,1)S(1)} %fusion.72) | copy-start | bytes 871
  32.6 18.5 %copy-start.12 = (pred[257]{0:T(512)(128)(4,1)}, pred[257]{0:T(512)(128)(4,1)S(1)}, u32[]{:S(2)}) copy-start(pred[257]{0:T(512)(128)(4,1)S(1)} %fusion.73) | copy-start | bytes 775
  32.6 13.9 %collective-permute-start.4 = (f32[1,290,258]{2,0,1:T(1,128)S(1)}, f32[1,290,258]{2,0,1:T(1,128)S(1)}, u32[]{:S(2)}, u32[]{:S(2)}) collective-permute-start(f32[1,290,258]{2,0,1:T(1,128)S(1)} %get-tuple-element.31), channel_id=1, source_target_pairs={{1,0},{2,1},{3,2},{5,4},{6,5},{7,6},{9,8},{10,9},{11,10},{13,12},{... | collective-permute-start | bytes 897848 | tf_op jit(solution)/shard_map/ppermute | solution.py:25
  34.2 17.0 %copy-start.16 = (pred[5]{0:T(512)(128)(4,1)}, pred[5]{0:T(512)(128)(4,1)S(1)}, u32[]{:S(2)}) copy-start(pred[5]{0:T(512)(128)(4,1)S(1)} %compare_and_fusion) | copy-start | bytes 19
  46.5 6.8 %slice-start = ((s8[4718592]{0:T(1024)(128)(4,1)}), s8[4194304]{0:T(1024)(128)(4,1)S(1)}, s32[]{:S(2)}) async-start(s8[4718592]{0:T(1024)(128)(4,1)} %bitcast.86), calls=%async_computation.2 | async-start | bytes 8388608
  51.1 2.2 slice-start.1
  51.1 2.2 copy-start
  51.2 2.2 copy-start.1
  51.2 2.2 copy-start.7
  51.2 2.2 copy-start.15
  66.3 3.8 %collective-permute-start.6 = (f32[4,1,256]{2,0,1:T(4,128)S(1)}, f32[4,1,256]{2,0,1:T(4,128)S(1)}, u32[]{:S(2)}, u32[]{:S(2)}) collective-permute-start(f32[4,1,256]{2,0,1:T(4,128)S(1)} %get-tuple-element.41), channel_id=1, source_target_pairs={{0,16},{1,17},{2,18},{3,19},{4,20},{5,21},{6,22},{7,23},{8,24},{9,... | collective-permute-start | bytes 12296 | tf_op jit(solution)/shard_map/ppermute | solution.py:22
  68.8 5.5 %collective-permute-start.7 = (f32[4,1,256]{2,0,1:T(4,128)S(1)}, f32[4,1,256]{2,0,1:T(4,128)S(1)}, u32[]{:S(2)}, u32[]{:S(2)}) collective-permute-start(f32[4,1,256]{2,0,1:T(4,128)S(1)} %get-tuple-element.42), channel_id=1, source_target_pairs={{16,0},{17,1},{18,2},{19,3},{20,4},{21,5},{22,6},{23,7},{24,8},{25... | collective-permute-start | bytes 12296 | tf_op jit(solution)/shard_map/ppermute | solution.py:25
  75.8 3.4 %collective-permute-start.8 = (f32[4,290,1]{1,0,2:T(4,128)}, f32[4,290,1]{1,0,2:T(4,128)S(1)}, u32[]{:S(2)}, u32[]{:S(2)}) collective-permute-start(f32[4,290,1]{1,0,2:T(4,128)} %copy.56), channel_id=1, source_target_pairs={{0,4},{4,8},{8,12},{1,5},{5,9},{9,13},{2,6},{6,10},{10,14},{3,7},{... | collective-permute-start | bytes 13928 | tf_op jit(solution)/shard_map/ppermute | solution.py:22
  77.5 3.7 %collective-permute-start.9 = (f32[4,290,1]{1,0,2:T(4,128)S(1)}, f32[4,290,1]{1,0,2:T(4,128)}, u32[]{:S(2)}, u32[]{:S(2)}) collective-permute-start(f32[4,290,1]{1,0,2:T(4,128)S(1)} %copy.57), channel_id=1, source_target_pairs={{4,0},{8,4},{12,8},{5,1},{9,5},{13,9},{6,2},{10,6},{14,10},{7,3},{... | collective-permute-start | bytes 13928 | tf_op jit(solution)/shard_map/ppermute | solution.py:25
  87.5 17.4 %copy-start.10 = (pred[289]{0:T(512)(128)(4,1)S(1)}, pred[289]{0:T(512)(128)(4,1)}, u32[]{:S(2)}) copy-start(pred[289]{0:T(512)(128)(4,1)} %copy-done.9) | copy-start | bytes 871
  87.5 17.4 %copy-start.13 = (pred[257]{0:T(512)(128)(4,1)S(1)}, pred[257]{0:T(512)(128)(4,1)}, u32[]{:S(2)}) copy-start(pred[257]{0:T(512)(128)(4,1)} %copy-done.12) | copy-start | bytes 775
  87.6 17.4 %copy-start.17 = (pred[5]{0:T(512)(128)(4,1)S(1)}, pred[5]{0:T(512)(128)(4,1)}, u32[]{:S(2)}) copy-start(pred[5]{0:T(512)(128)(4,1)} %copy-done.16) | copy-start | bytes 19
  87.6 12.7 %collective-permute-start.11 = (f32[1,290,258]{2,0,1:T(1,128)S(1)}, f32[1,290,258]{2,0,1:T(1,128)S(1)}, u32[]{:S(2)}, u32[]{:S(2)}) collective-permute-start(f32[1,290,258]{2,0,1:T(1,128)S(1)} %get-tuple-element.30), channel_id=1, source_target_pairs={{0,1},{1,2},{2,3},{4,5},{5,6},{6,7},{8,9},{9,10},{10,11},{12,13},{... | collective-permute-start | bytes 897848 | tf_op jit(solution)/shard_map/ppermute | solution.py:22
  91.1 13.9 %collective-permute-start.10 = (f32[1,290,258]{2,0,1:T(1,128)S(1)}, f32[1,290,258]{2,0,1:T(1,128)S(1)}, u32[]{:S(2)}, u32[]{:S(2)}) collective-permute-start(f32[1,290,258]{2,0,1:T(1,128)S(1)} %get-tuple-element.29), channel_id=1, source_target_pairs={{1,0},{2,1},{3,2},{5,4},{6,5},{7,6},{9,8},{10,9},{11,10},{13,12},{... | collective-permute-start | bytes 897848 | tf_op jit(solution)/shard_map/ppermute | solution.py:25
  109.5 2.2 copy-start.4
  115.0 3.0 collective-permute-start.12
  116.6 5.5 %collective-permute-start.13 = (f32[4,1,256]{2,0,1:T(4,128)S(1)}, f32[4,1,256]{2,0,1:T(4,128)S(1)}, u32[]{:S(2)}, u32[]{:S(2)}) collective-permute-start(f32[4,1,256]{2,0,1:T(4,128)S(1)} %get-tuple-element.40), channel_id=1, source_target_pairs={{16,0},{17,1},{18,2},{19,3},{20,4},{21,5},{22,6},{23,7},{24,8},{25... | collective-permute-start | bytes 12296 | tf_op jit(solution)/shard_map/ppermute | solution.py:25
  124.9 3.0 collective-permute-start.14
  126.6 4.0 %collective-permute-start.15 = (f32[4,290,1]{1,0,2:T(4,128)S(1)}, f32[4,290,1]{1,0,2:T(4,128)S(1)}, u32[]{:S(2)}, u32[]{:S(2)}) collective-permute-start(f32[4,290,1]{1,0,2:T(4,128)S(1)} %copy.61), channel_id=1, source_target_pairs={{4,0},{8,4},{12,8},{5,1},{9,5},{13,9},{6,2},{10,6},{14,10},{7,3},{... | collective-permute-start | bytes 13928 | tf_op jit(solution)/shard_map/ppermute | solution.py:25
  131.7 25.9 %copy-start.6 = (f32[4,290,1]{2,0,1:T(4,128)S(1)}, f32[4,290,1]{2,0,1:T(4,128)}, u32[]{:S(2)}) copy-start(f32[4,290,1]{2,0,1:T(4,128)} %copy.63) | copy-start | bytes 13924
  138.4 19.2 %collective-permute-start.17 = (f32[1,290,258]{2,0,1:T(1,128)S(1)}, f32[1,290,258]{2,0,1:T(1,128)S(1)}, u32[]{:S(2)}, u32[]{:S(2)}) collective-permute-start(f32[1,290,258]{2,0,1:T(1,128)S(1)} %get-tuple-element.28), channel_id=1, source_target_pairs={{0,1},{1,2},{2,3},{4,5},{5,6},{6,7},{8,9},{9,10},{10,11},{12,13},{... | collective-permute-start | bytes 897848 | tf_op jit(solution)/shard_map/ppermute | solution.py:22
  141.9 17.2 %collective-permute-start.16 = (f32[1,290,258]{2,0,1:T(1,128)S(1)}, f32[1,290,258]{2,0,1:T(1,128)S(1)}, u32[]{:S(2)}, u32[]{:S(2)}) collective-permute-start(f32[1,290,258]{2,0,1:T(1,128)S(1)} %get-tuple-element.27), channel_id=1, source_target_pairs={{1,0},{2,1},{3,2},{5,4},{6,5},{7,6},{9,8},{10,9},{11,10},{13,12},{... | collective-permute-start | bytes 897848 | tf_op jit(solution)/shard_map/ppermute | solution.py:25
  157.6 1.6 copy-start.11
  157.6 1.6 copy-start.14
  157.6 1.6 copy-start.18
  159.2 10.4 %slice-start.2 = ((s8[4718592]{0:T(1024)(128)(4,1)}), s8[4194304]{0:T(1024)(128)(4,1)S(1)}, s32[]{:S(2)}) async-start(s8[4718592]{0:T(1024)(128)(4,1)} %bitcast.89), calls=%async_computation.4 | async-start | bytes 8388608
  164.0 2.2 copy-start.5
  164.0 5.6 %slice-start.3 = ((s8[4718592]{0:T(1024)(128)(4,1)}), s8[524288]{0:T(1024)(128)(4,1)S(1)}, s32[]{:S(2)}) async-start(s8[4718592]{0:T(1024)(128)(4,1)} %bitcast.89), calls=%async_computation.5 | async-start | bytes 1048576
  166.2 3.5 %copy-start.2 = (f32[4,288,256]{2,1,0:T(8,128)S(1)}, f32[4,288,256]{2,1,0:T(8,128)}, u32[]{:S(2)}) copy-start(f32[4,288,256]{2,1,0:T(8,128)} %param.6) | copy-start | bytes 3538948
  169.7 43.9 %copy-start.3 = (f32[4,288,256]{2,1,0:T(8,128)S(1)}, f32[4,288,256]{2,1,0:T(8,128)}, u32[]{:S(2)}) copy-start(f32[4,288,256]{2,1,0:T(8,128)} %param.6) | copy-start | bytes 3538948
  213.6 15.0 %copy-start.8 = (f32[16,4]{0,1:T(4,128)}, f32[16,4]{0,1:T(4,128)S(1)}, u32[]{:S(2)}) copy-start(f32[16,4]{0,1:T(4,128)S(1)} %fusion.56) | copy-start | bytes 772
Sparse Core Ops, SparseCore 0:
  220.3 83.9 reduce-scatter.1
where the time goes:
time: 322 us; the launch traced here: 317 us
  waiting for transfers between devices  99.1 us (31%)
  other arithmetic  57.9 us (18%)
  matrix products  49 us (15%)
  blocking collectives  36.3 us (11%)
  starting transfers between devices  36.1 us (11%)
  local copies, waits for them, and re-layouts  23.6 us (7%)
  between operations  15.2 us (5%)
    reduce_scatter x1, waiting for transfers between devices, local(): lax.psum_scatter(total_part, 'frame', scatter_dimension=1, tiled=True)  59.6 us
    psum x1, blocking collectives, local(): gram_sum, cross_sum = lax.psum((gram_part, cross_part), ('row', 'col'))  24.6 us
    ppermute x9, waiting for transfers between devices, with_halo(): lax.ppermute(lax.slice_in_dim(block, 0, width, axis=dim), axis, backward)  24 us
    ppermute x9, starting transfers between devices, with_halo(): lax.ppermute(lax.slice_in_dim(block, block.shape[dim] - width, None, axis...  23.6 us
    mul x6, other arithmetic, descend(): fluxes = [slope_part * weight for slope_part in slopes]  20.3 us
    ppermute x9, waiting for transfers between devices, with_halo(): lax.ppermute(lax.slice_in_dim(block, block.shape[dim] - width, None, axis...  15.5 us
    slice x3, other arithmetic, with_halo(): lax.slice_in_dim(block, 0, width, axis=dim)  15.2 us
    dot_general x1, matrix products, local(): gram_part = jnp.dot(flat_basis, flat_basis.T, precision=highest)  14.2 us
  transfers between devices with their start and end apart: 19, of which 11 were waited for; matrix products, arithmetic and copies ran while one was open for 11% of the time, Pallas kernels for 0%

commit v1 on v0

--- a/solution.py
+++ b/solution.py
@@ -1,6 +1,10 @@
+import functools
+
 import jax
 import jax.numpy as jnp
 from jax import lax
+from jax.experimental import pallas as pl
+from jax.experimental.pallas import tpu as pltpu
 from jax.sharding import PartitionSpec as P
 
 PASSES = 3
@@ -115,6 +119,508 @@
     return (shrunk, coeff_rows.T, new_basis.reshape(rank_size, owned_rows, cols_here))
 
 
+MESH = pl.DeviceIdType.MESH
+CHUNK = 32
+
+
+def eliminate(matrix, size):
+    lanes = lax.broadcasted_iota(jnp.int32, matrix.shape, 1)
+    rows = lax.broadcasted_iota(jnp.int32, matrix.shape, 0)
+    for k in range(size):
+        pivot = matrix[k : k + 1, k : k + 1]
+        scaled = matrix[k : k + 1, :] / pivot
+        column = jnp.sum(jnp.where(lanes == k, matrix, 0.0), axis=1, keepdims=True)
+        matrix = jnp.where(rows == k, scaled, matrix - column * scaled)
+    return matrix
+
+
+def kernel(
+    sizes, coeff_ref, video_hbm, mult_hbm, fore_hbm, basis_hbm,
+    shrunk_hbm, rows_out, new_basis_hbm,
+    field, video, mult, basis, anchor, target, result, owned,
+    packed, arrived, corner, edge_next, edge_flux, first_cols,
+    sums, parts, shares, square, table, table_smem,
+    in_sems, out_sems, halo_send, halo_recv, part_send, part_recv,
+    share_send, share_recv, move_send, move_recv, small_sem, barrier_own,
+):
+    F, H, W, rank, nr, nc, nz = sizes
+    r = lax.axis_index("row")
+    c = lax.axis_index("col")
+    z = lax.axis_index("frame")
+    own = H // nz
+
+    def inside(dr, dc, dz):
+        ok = None
+        for at, step, count in ((r, dr, nr), (c, dc, nc), (z, dz, nz)):
+            if step != 0:
+                test = (at + step >= 0) & (at + step < count)
+                ok = test if ok is None else ok & test
+        return ok
+
+    loads = []
+    for i, (src, dst) in enumerate(
+        (
+            (fore_hbm, field.at[0, 1 : F + 1, 8 : H + 8, :]),
+            (basis_hbm, basis),
+            (video_hbm, video),
+            (mult_hbm, mult),
+        )
+    ):
+        copy = pltpu.make_async_copy(src, dst, in_sems.at[i])
+        copy.start()
+        loads.append(copy)
+
+    barrier = pltpu.get_barrier_semaphore()
+    for d in range(1, nr * nc):
+        other = lax.rem(r * nc + c + d, nr * nc)
+        pl.semaphore_signal(
+            barrier, inc=1, device_id=(other // nc, lax.rem(other, nc), z), device_id_type=MESH
+        )
+    for d in range(1, nz):
+        pl.semaphore_signal(
+            barrier, inc=1, device_id=(r, c, lax.rem(z + d, nz)), device_id_type=MESH
+        )
+    diagonals = ((1, 0, -1), (-1, 0, 1), (0, 1, -1), (0, -1, 1))
+    for step in diagonals:
+        @pl.when(inside(*step))
+        def _(step=step):
+            pl.semaphore_signal(
+                barrier,
+                inc=1,
+                device_id=(r + step[0], c + step[1], z + step[2]),
+                device_id_type=MESH,
+            )
+    expected = jnp.int32(nr * nc - 1 + nz - 1)
+    for step in diagonals:
+        expected = expected + inside(*step).astype(jnp.int32)
+    pl.semaphore_wait(barrier, expected)
+
+    lane_h = lax.broadcasted_iota(jnp.int32, (H, 128), 1)
+
+    def pack_columns(k):
+        for side in range(2):
+            tile = jnp.zeros((H, 128), jnp.float32)
+            for f in range(F):
+                at = 0 if side == 0 else W - 1
+                lanes = field[k, f + 1, 8 : H + 8, (at // 128) * 128 : (at // 128) * 128 + 128]
+                column = lanes[:, at % 128 : at % 128 + 1]
+                tile = jnp.where(lane_h == f, column, tile)
+            if side == 0:
+                first_cols[...] = tile
+            packed[k, side] = tile.T[:8, :]
+
+    def halo_list(k):
+        fk = field.at[k]
+        mid = slice(1, F + 1)
+        return (
+            (fk.at[F, 8 : H + 8, :], fk.at[0, 8 : H + 8, :], (0, 0, 1)),
+            (fk.at[1, 8 : H + 8, :], fk.at[F + 1, 8 : H + 8, :], (0, 0, -1)),
+            (packed.at[k, 0], arrived.at[k, 0], (0, -1, 0)),
+            (packed.at[k, 1], arrived.at[k, 1], (0, 1, 0)),
+            (packed.at[k, 0], arrived.at[k, 2], (0, -1, 1)),
+            (packed.at[k, 1], arrived.at[k, 3], (0, 1, -1)),
+            (fk.at[mid, H : H + 8, :], fk.at[mid, 0:8, :], (1, 0, 0)),
+            (fk.at[mid, 8:16, :], fk.at[mid, H + 8 : H + 16, :], (-1, 0, 0)),
+            (fk.at[F, 8:16, :], fk.at[0, H + 8 : H + 16, :], (-1, 0, 1)),
+            (fk.at[1, H : H + 8, :], fk.at[F + 1, 0:8, :], (1, 0, -1)),
+            (fk.at[mid, H : H + 8, 0:128], corner.at[k, 0], (1, -1, 0)),
+            (fk.at[mid, 8:16, W - 128 : W], corner.at[k, 1], (-1, 1, 0)),
+        )
+
+    def halo_copy(k, i, src, dst, step):
+        return pltpu.make_async_remote_copy(
+            src_ref=src, dst_ref=dst,
+            send_sem=halo_send.at[k, i], recv_sem=halo_recv.at[k, i],
+            device_id=(r + step[0], c + step[1], z + step[2]), device_id_type=MESH,
+        )
+
+    def send_halos(k):
+        for i, (src, dst, step) in enumerate(halo_list(k)):
+            @pl.when(inside(*step))
+            def _(i=i, src=src, dst=dst, step=step):
+                halo_copy(k, i, src, dst, step).start()
+
+    def wait_halos(k):
+        for i, (src, dst, step) in enumerate(halo_list(k)):
+            @pl.when(inside(*(-s for s in step)))
+            def _(i=i, src=src, dst=dst, step=step):
+                halo_copy(k, i, src, dst, step).wait_recv()
+
+    def finish_sends(k):
+        for i, (src, dst, step) in enumerate(halo_list(k)):
+            @pl.when(inside(*step))
+            def _(i=i, src=src, dst=dst, step=step):
+                halo_copy(k, i, src, dst, step).wait_send()
+
+    def prepare_columns(k):
+        tall = jnp.concatenate([arrived[k, 0], jnp.zeros((120, H), jnp.float32)], axis=0).T
+        edge = jnp.concatenate([arrived[k, 2], jnp.zeros((120, H), jnp.float32)], axis=0).T
+        tile = jnp.where(lane_h == 0, edge[:, F - 1 : F], pltpu.roll(tall, 1, 1))
+        edge_next[8 : H + 8, :] = tile
+        lane8 = lax.broadcasted_iota(jnp.int32, (8, 128), 1)
+        top = jnp.zeros((8, 128), jnp.float32)
+        bottom = jnp.zeros((1, 128), jnp.float32)
+        for f in range(F):
+            top = jnp.where(lane8 == f + 1, corner[k, 0, f][:, 0:1], top)
+            bottom = jnp.where(lane8[:1] == f, corner[k, 1, f][0:1, 127:128], bottom)
+        edge_next[0:8, :] = top
+        edge_next[H + 8 : H + 16, :] = jnp.zeros((8, 128), jnp.float32)
+        here = jnp.concatenate([arrived[k, 1], jnp.zeros((120, H), jnp.float32)], axis=0).T
+        edge = jnp.concatenate([arrived[k, 3], jnp.zeros((120, H), jnp.float32)], axis=0).T
+        ahead = jnp.where(lane_h == F - 1, edge[:, 0:1], pltpu.roll(here, 127, 1))
+        slope0 = jnp.where((lane_h == F - 1) & (z == nz - 1), 0.0, ahead - here)
+        row_h = lax.broadcasted_iota(jnp.int32, (H, 128), 0)
+        below = jnp.where(row_h == H - 1, bottom, pltpu.roll(here, H - 1, 0))
+        slope1 = jnp.where((row_h == H - 1) & (r == nr - 1), 0.0, below - here)
+        slope2 = first_cols[...] - here
+        weight = lax.rsqrt(smooth_floor + slope0 * slope0 + slope1 * slope1 + slope2 * slope2)
+        edge_flux[...] = jnp.where(c == 0, 0.0, slope2 * weight)
+
+    def sweep(k, last):
+        @pl.loop(0, H // CHUNK)
+        def _(step):
+            start = pl.multiple_of(step * CHUNK, 8)
+            R = CHUNK
+            lane_t = lax.broadcasted_iota(jnp.int32, (R + 8, 128), 1)
+            row_t = lax.broadcasted_iota(jnp.int32, (R + 8, W), 0) + (r * H + start - 8)
+            lane_w = lax.broadcasted_iota(jnp.int32, (R + 8, W), 1)
+            blocked = (row_t < 0) | (row_t >= nr * H - 1)
+            columns = edge_next[pl.ds(start, R + 8), :]
+            fluxes_in = edge_flux[pl.ds(start, R), :]
+            now = field[k, 0, pl.ds(start, R + 16), :]
+            flux0_before = None
+            for f in range(-1, F):
+                after = field[k, f + 2, pl.ds(start, R + 16), :]
+                here = now[: R + 8]
+                below = pltpu.roll(now, R + 15, 0)[: R + 8]
+                ahead = after[: R + 8]
+                wall = columns[:, f + 1 : f + 2]
+                beyond = jnp.where(c == nc - 1, here, jnp.broadcast_to(wall, here.shape))
+                right = jnp.where(lane_w == W - 1, beyond, pltpu.roll(here, W - 1, 1))
+                slope0 = ahead - here
+                if f == F - 1:
+                    slope0 = jnp.where(z == nz - 1, 0.0, slope0)
+                slope1 = jnp.where(blocked, 0.0, below - here)
+                slope2 = right - here
+                weight = lax.rsqrt(
+                    smooth_floor + slope0 * slope0 + slope1 * slope1 + slope2 * slope2
+                )
+                flux0 = (slope0 * weight)[8:]
+                if f < 0:
+                    flux0 = jnp.where(z == 0, 0.0, flux0)
+                else:
+                    flux1 = jnp.where(row_t < 0, 0.0, slope1 * weight)
+                    flux2 = (slope2 * weight)[8:]
+                    above = pltpu.roll(flux1, 1, 0)[8:]
+                    left = jnp.where(
+                        lane_w[8:] == 0,
+                        jnp.broadcast_to(fluxes_in[:, f : f + 1], flux2.shape),
+                        pltpu.roll(flux2, 1, 1),
+                    )
+                    spread = flux0 - flux0_before + (flux1[8:] - above) + (flux2 - left)
+                    center = here[8:]
+                    at = pl.ds(start, R)
+                    value = center + relax_rate * (
+                        target[f, at, :] - center + smooth_weight * spread
+                    )
+                    if last:
+                        shrunk = value - jnp.clip(value, -shrink_level, shrink_level)
+                        result[f, at, :] = shrunk
+                        anchor[f, at, :] = anchor[f, at, :] - shrunk
+                    else:
+                        field[k + 1, f + 1, pl.ds(start + 8, R), :] = value
+                flux0_before = flux0
+                now = after
+
+    def products(left_of, right_of, lefts, rights, store):
+        zero = jnp.zeros((8, 128), jnp.float32)
+
+        def body(step, totals):
+            rows = pl.ds(pl.multiple_of(step * 8, 8), 8)
+            a = [left_of[i, rows, :] for i in lefts]
+            b = [right_of[j, rows, :] for j in rights]
+            out = []
+            for x in range(len(lefts)):
+                for y in range(len(rights)):
+                    prod = a[x] * b[y]
+                    total = totals[len(out)]
+                    for w in range(W // 128):
+                        total = total + prod[:, w * 128 : w * 128 + 128]
+                    out.append(total)
+            return tuple(out)
+
+        totals = lax.fori_loop(0, H // 8, body, (zero,) * (len(lefts) * len(rights)), unroll=2)
+        n = 0
+        for i in lefts:
+            for j in rights:
+                store(i, j, jnp.sum(totals[n], axis=0, keepdims=True))
+                n += 1
+
+    loads[0].wait()
+    pack_columns(0)
+    send_halos(0)
+    loads[1].wait()
+
+    def store_gram(i, j, value):
+        sums[j, i : i + 1, :] = value
+        if i // 4 != j // 4:
+            sums[i, j : j + 1, :] = value
+
+    for i in range(0, rank, 4):
+        for j in range(i, rank, 4):
+            products(basis, basis, range(i, i + 4), range(j, j + 4), store_gram)
+
+    loads[2].wait()
+    loads[3].wait()
+
+    @pl.loop(0, H // 8)
+    def _(step):
+        rows = pl.ds(pl.multiple_of(step * 8, 8), 8)
+        totals = [None] * F
+        for q in range(rank):
+            plane = basis[q, rows, :]
+            for f in range(F):
+                term = coeff_ref[f, q] * plane
+                totals[f] = term if totals[f] is None else totals[f] + term
+        for f in range(F):
+            lifted = dual_scale * mult[f, rows, :]
+            anchor[f, rows, :] = video[f, rows, :] + lifted
+            target[f, rows, :] = video[f, rows, :] - totals[f] + lifted
+
+    for k in range(PASSES):
+        wait_halos(k)
+        prepare_columns(k)
+        sweep(k, k == PASSES - 1)
+        if k < PASSES - 1:
+            pack_columns(k + 1)
+            send_halos(k + 1)
+
+    out_copy = pltpu.make_async_copy(result, shrunk_hbm, out_sems.at[0])
+    out_copy.start()
+
+    def move(d):
+        there = lax.rem(z + d, nz)
+        rows = pl.ds(pl.multiple_of(there * own, 8), own)
+        return pltpu.make_async_remote_copy(
+            src_ref=anchor.at[:, rows, :], dst_ref=owned.at[pl.ds(z * F, F)],
+            send_sem=move_send.at[d], recv_sem=move_recv.at[d],
+            device_id=(r, c, there), device_id_type=MESH,
+        )
+
+    def take(d):
+        source = lax.rem(z - d + nz, nz)
+        rows = pl.ds(pl.multiple_of(z * own, 8), own)
+        return pltpu.make_async_remote_copy(
+            src_ref=anchor.at[:, rows, :], dst_ref=owned.at[pl.ds(source * F, F)],
+            send_sem=move_send.at[d], recv_sem=move_recv.at[d],
+            device_id=(r, c, source), device_id_type=MESH,
+        )
+
+    for d in range(1, nz):
+        move(d).start()
+    my_rows = pl.ds(pl.multiple_of(z * own, 8), own)
+    keep = pltpu.make_async_copy(
+        anchor.at[:, my_rows, :], owned.at[pl.ds(z * F, F)], small_sem.at[0]
+    )
+    keep.start()
+
+    def store_cross(i, j, value):
+        sums[rank + j, i : i + 1, :] = value
+
+    for i in range(0, rank, 4):
+        products(basis, anchor, range(i, i + 4), range(F), store_cross)
+
+    lane_r = lax.broadcasted_iota(jnp.int32, (rank, 128), 1)
+    row_r = lax.broadcasted_iota(jnp.int32, (rank, 128), 0)
+    part = jnp.zeros((rank, 128), jnp.float32)
+    for q in range(rank + F):
+        part = jnp.where(lane_r == q, jnp.sum(sums[q], axis=1, keepdims=True), part)
+    group = nr * nc
+    me = r * nc + c
+    parts[me] = part
+
+    def share_part(d):
+        other = lax.rem(me + d, group)
+        return pltpu.make_async_remote_copy(
+            src_ref=parts.at[me], dst_ref=parts.at[me],
+            send_sem=part_send.at[d], recv_sem=part_recv.at[d],
+            device_id=(other // nc, lax.rem(other, nc), z), device_id_type=MESH,
+        )
+
+    def take_part(d):
+        other = lax.rem(me - d + group, group)
+        return pltpu.make_async_remote_copy(
+            src_ref=parts.at[me], dst_ref=parts.at[other],
+            send_sem=part_send.at[d], recv_sem=part_recv.at[d],
+            device_id=(other // nc, lax.rem(other, nc), z), device_id_type=MESH,
+        )
+
+    for d in range(1, group):
+        share_part(d).start()
+    for d in range(1, group):
+        take_part(d).wait_recv()
+    total = parts[0]
+    for i in range(1, group):
+        total = total + parts[i]
+    pixel_ridge = ridge_share * H * W * group
+    diagonal = lane_r == row_r
+    before = jnp.zeros((rank, 128), jnp.float32)
+    for q in range(rank):
+        for f in range(F):
+            before = jnp.where((row_r == q) & (lane_r == rank + f), coeff_ref[f, q], before)
+    total = total + pixel_ridge * (jnp.where(diagonal, 1.0, 0.0) + before)
+    solved = eliminate(total, rank)
+    shares[z] = solved
+    rows_out[...] = solved
+
+    def share_rows(d):
+        return pltpu.make_async_remote_copy(
+            src_ref=shares.at[z], dst_ref=shares.at[z],
+            send_sem=share_send.at[d], recv_sem=share_recv.at[d],
+            device_id=(r, c, lax.rem(z + d, nz)), device_id_type=MESH,
+        )
+
+    def take_rows(d):
+        source = lax.rem(z - d + nz, nz)
+        return pltpu.make_async_remote_copy(
+            src_ref=shares.at[z], dst_ref=shares.at[source],
+            send_sem=share_send.at[d], recv_sem=share_recv.at[d],
+            device_id=(r, c, source), device_id_type=MESH,
+        )
+
+    for d in range(1, nz):
+        share_rows(d).start()
+    for d in range(1, nz):
+        take_rows(d).wait_recv()
+    frames = F * nz
+    wide = jnp.zeros((rank, 128), jnp.float32)
+    for i in range(nz):
+        placed = shares[i] if i == 0 else pltpu.roll(shares[i], i * F, 1)
+        wide = jnp.where(
+            (lane_r >= rank + i * F) & (lane_r < rank + (i + 1) * F), placed, wide
+        )
+    square[...] = jnp.zeros_like(square)
+    square[0:rank, :] = wide
+    gram = lax.dot_general(
+        wide, square[...], (((1,), (1,)), ((), ())),
+        precision=lax.Precision.HIGHEST, preferred_element_type=jnp.float32,
+    )
+    frame_ridge = ridge_share * frames
+    system = jnp.where(diagonal, gram + frame_ridge, gram) + wide
+    system = system + jnp.where(lane_r == row_r + rank + frames, frame_ridge, 0.0)
+    table[...] = eliminate(system, rank)
+    to_scalar = pltpu.make_async_copy(table, table_smem, small_sem.at[1])
+    to_scalar.start()
+    to_scalar.wait()
+    keep.wait()
+    for d in range(1, nz):
+        take(d).wait_recv()
+
+    @pl.loop(0, own // 8)
+    def _(step):
+        rows = pl.ds(pl.multiple_of(step * 8, 8), 8)
+        old = pl.ds(pl.multiple_of(z * own + step * 8, 8), 8)
+
+        for half in range(0, rank, 8):
+            totals = [None] * 8
+            for f in range(frames + rank):
+                plane = owned[f, rows, :] if f < frames else basis[f - frames, old, :]
+                for q in range(8):
+                    term = table_smem[half + q, rank + f] * plane
+                    totals[q] = term if totals[q] is None else totals[q] + term
+            for q in range(8):
+                target_rows = totals[q]
+                barrier_own[half + q, rows, :] = target_rows
+
+    last_copy = pltpu.make_async_copy(barrier_own, new_basis_hbm, out_sems.at[1])
+    last_copy.start()
+    for k in range(PASSES):
+        finish_sends(k)
+    for d in range(1, nz):
+        move(d).wait_send()
+        share_rows(d).wait_send()
+    for d in range(1, group):
+        share_part(d).wait_send()
+    out_copy.wait()
+    last_copy.wait()
+
+
+def whole_kernel(video, multiplier, foreground, basis, coefficients):
+    F, H, W = video.shape
+    rank = basis.shape[0]
+    nr, nc, nz = (lax.axis_size(name) for name in ("row", "col", "frame"))
+    f32 = jnp.float32
+    own = H // nz
+    group = nr * nc
+    vmem = pltpu.VMEM
+    dma = pltpu.SemaphoreType.DMA
+    shrunk, rows, new_basis = pl.pallas_call(
+        functools.partial(kernel, (F, H, W, rank, nr, nc, nz)),
+        out_shape=(
+            jax.ShapeDtypeStruct((F, H, W), f32),
+            jax.ShapeDtypeStruct((rank, 128), f32),
+            jax.ShapeDtypeStruct((rank, own, W), f32),
+        ),
+        in_specs=[pl.BlockSpec(memory_space=pltpu.SMEM)]
+        + [pl.BlockSpec(memory_space=pl.ANY)] * 4,
+        out_specs=(
+            pl.BlockSpec(memory_space=pl.ANY),
+            pl.BlockSpec(memory_space=pltpu.VMEM),
+            pl.BlockSpec(memory_space=pl.ANY),
+        ),
+        scratch_shapes=[
+            vmem((PASSES, F + 2, H + 16, W), f32),
+            vmem((F, H, W), f32),
+            vmem((F, H, W), f32),
+            vmem((rank, H, W), f32),
+            vmem((F, H, W), f32),
+            vmem((F, H, W), f32),
+            vmem((F, H, W), f32),
+            vmem((F * nz, own, W), f32),
+            vmem((PASSES, 2, 8, H), f32),
+            vmem((PASSES, 4, 8, H), f32),
+            vmem((PASSES, 2, F, 8, 128), f32),
+            vmem((H + 16, 128), f32),
+            vmem((H, 128), f32),
+            vmem((H, 128), f32),
+            vmem((rank + F, rank, 128), f32),
+            vmem((group, rank, 128), f32),
+            vmem((nz, rank, 128), f32),
+            vmem((128, 128), f32),
+            vmem((rank, 128), f32),
+            pltpu.SMEM((rank, 128), f32),
+            dma((4,)),
+            dma((2,)),
+            dma((PASSES, 12)),
+            dma((PASSES, 12)),
+            dma((group,)),
+            dma((group,)),
+            dma((nz,)),
+            dma((nz,)),
+            dma((nz,)),
+            dma((nz,)),
+            dma((2,)),
+            vmem((rank, own, W), f32),
+        ],
+        compiler_params=pltpu.CompilerParams(
+            collective_id=0, has_side_effects=True, vmem_limit_bytes=60 * 1024 * 1024
+        ),
+    )(coefficients, video, multiplier, foreground, basis)
+    return (shrunk, rows[:, rank : rank + F].T, new_basis)
+
+
+def body(video, multiplier, foreground, basis, coefficients):
+    F, H, W = video.shape
+    rank = basis.shape[0]
+    nz = lax.axis_size("frame")
+    fits = (
+        H % nz == 0 and (H // nz) % 8 == 0 and H % CHUNK == 0 and W % 128 == 0
+        and F <= 8 and rank % 8 == 0 and 2 * rank + F * nz <= 128
+    )
+    run = whole_kernel if fits else local
+    return run(video, multiplier, foreground, basis, coefficients)
+
+
 def solution(mesh):
     placed = (
         P("frame", "row", "col"),
@@ -124,7 +630,7 @@
         P("frame", None),
     )
     return jax.shard_map(
-        local,
+        body,
         mesh=mesh,
         in_specs=placed,
         out_specs=(P("frame", "row", "col"), P("frame", None), P(None, ("row", "frame"), "col")),

time: 322 us -> 88.4 us (0.27); the launches traced: 317 us -> 88.2 us
  waiting for transfers between devices: 99.1 us -> 0 us
  Pallas kernels: 0 us -> 82.6 us
  other arithmetic: 57.9 us -> 0 us
  matrix products: 49 us -> 0 us
  blocking collectives: 36.3 us -> 0 us
  starting transfers between devices: 36.1 us -> 0 us
  local copies, waits for them, and re-layouts: 23.6 us -> 4.9 us
  between operations: 15.2 us -> 0.64 us
    pallas_call x0 -> x1, Pallas kernels: none -> 82.6 us  [whole_kernel(): pl.pallas_call(functools.partial(kernel, (F, H, W, rank, nr, nc, nz)), ou...]
    reduce_scatter x1 -> x0, waiting for transfers between devices: 59.6 us -> none  [local(): lax.psum_scatter(total_part, 'frame', scatter_dimension=1, tiled=True)]
    dot_general x5 -> x0, matrix products: 44.1 us -> none  [the longest x1 14.2 us: local(): gram_part = jnp.dot(flat_basis, flat_basis.T, precision=highest)]
    ppermute x18 -> x0, waiting for transfers between devices: 39.5 us -> none  [the longest x9 24 us: with_halo(): lax.ppermute(lax.slice_in_dim(block, 0, width, axis=dim), axis, backward)]
    psum x2 -> x0, blocking collectives: 36.3 us -> none  [the longest x1 24.6 us: local(): gram_sum, cross_sum = lax.psum((gram_part, cross_part), ('row', 'col'))]
    ppermute x18 -> x0, starting transfers between devices: 36 us -> none  [the longest x9 23.6 us: with_halo(): lax.ppermute(lax.slice_in_dim(block, block.shape[dim] - width, None, axis...]
    mul x6 -> x0, other arithmetic: 20.3 us -> none  [descend(): fluxes = [slope_part * weight for slope_part in slopes]]
    slice x3 -> x0, other arithmetic: 15.2 us -> none  [with_halo(): lax.slice_in_dim(block, 0, width, axis=dim)]
  transfers between devices with their start and end apart: 19 -> 0, of which waited for: 11 -> 0; matrix products, arithmetic and copies ran while one was open for 11% -> 0% of each run, Pallas kernels for 0% -> 0%
where the time goes in v1:
time: 88.4 us; the launch traced here: 88.2 us
  Pallas kernels  82.6 us (93%)
  local copies, waits for them, and re-layouts  4.9 us (6%)
    pallas_call x1, Pallas kernels, whole_kernel(): pl.pallas_call(functools.partial(kernel, (F, H, W, rank, nr, nc, nz)), ou...  82.6 us
    unnamed x5, local copies, waits for them, and re-layouts  4.13 us

profile of v1, /device:TPU:0, one launch (start us, length us, event | category | flops | bytes accessed | tf_op | source)
XLA Modules:
  0.0 88.2 jit_solution(8660827499384971734)
XLA Ops:
  0.6 82.6 %shard_map.76 = (f32[4,288,256]{2,1,0:T(8,128)}, f32[16,128]{1,0:T(8,128)}, f32[16,72,256]{2,1,0:T(8,128)}) custom-call(f32[4,16]{1,0:T(4,128)} %coeff_ref.1, f32[4,288,256]{2,1,0:T(8,128)} %video_hbm.1, f32[4,288,256]{2,1,0:T(8,128)} %mult_hbm.1, f32[4,288,256]{2,1,0:T(8,128)} %fore_hbm.1, f32[16,288,256]{2,1,0:T(8,128)} %basis_hbm.1), custom_call_target="tpu_custom_call" | custom-call | tf_op jit(solution)/shard_map/pallas_call | solution.py:557
  83.3 0.8 slice_bitcast_fusion
  84.0 0.7 copy.8
  84.7 0.0 copy-start
  84.7 2.5 %copy.11 = f32[4,288,256]{2,1,0:T(8,128)} copy(f32[4,288,256]{2,1,0:T(8,128)} %get-tuple-element.15) | data formatting | bytes 2359296
  87.2 0.0 copy-done
  87.2 1.0 %copy.12 = f32[16,72,256]{2,1,0:T(8,128)} copy(f32[16,72,256]{2,1,0:T(8,128)S(1)} %copy-done) | data formatting | bytes 2359296
Async XLA Ops:
  84.7 2.5 %copy-start = (f32[16,72,256]{2,1,0:T(8,128)S(1)}, f32[16,72,256]{2,1,0:T(8,128)}, u32[]{:S(2)}) copy-start(f32[16,72,256]{2,1,0:T(8,128)} %get-tuple-element.17) | copy-start | bytes 3538948

commit v2 on v1

--- a/solution.py
+++ b/solution.py
@@ -120,7 +120,7 @@
 
 
 MESH = pl.DeviceIdType.MESH
-CHUNK = 32
+CHUNK = 24
 
 
 def eliminate(matrix, size):
@@ -213,8 +213,6 @@
         fk = field.at[k]
         mid = slice(1, F + 1)
         return (
-            (fk.at[F, 8 : H + 8, :], fk.at[0, 8 : H + 8, :], (0, 0, 1)),
-            (fk.at[1, 8 : H + 8, :], fk.at[F + 1, 8 : H + 8, :], (0, 0, -1)),
             (packed.at[k, 0], arrived.at[k, 0], (0, -1, 0)),
             (packed.at[k, 1], arrived.at[k, 1], (0, 1, 0)),
             (packed.at[k, 0], arrived.at[k, 2], (0, -1, 1)),
@@ -225,6 +223,14 @@
             (fk.at[1, H : H + 8, :], fk.at[F + 1, 0:8, :], (1, 0, -1)),
             (fk.at[mid, H : H + 8, 0:128], corner.at[k, 0], (1, -1, 0)),
             (fk.at[mid, 8:16, W - 128 : W], corner.at[k, 1], (-1, 1, 0)),
+        ) + tuple(
+            face
+            for b in range(nz)
+            for rows in (slice(8 + b * own, 8 + (b + 1) * own),)
+            for face in (
+                (fk.at[F, rows, :], fk.at[0, rows, :], (0, 0, 1)),
+                (fk.at[1, rows, :], fk.at[F + 1, rows, :], (0, 0, -1)),
+            )
         )
 
     def halo_copy(k, i, src, dst, step):
@@ -234,8 +240,11 @@
             device_id=(r + step[0], c + step[1], z + step[2]), device_id_type=MESH,
         )
 
-    def send_halos(k):
-        for i, (src, dst, step) in enumerate(halo_list(k)):
+    def send_halos(k, which):
+        every = halo_list(k)
+        for i in which:
+            src, dst, step = every[i]
+
             @pl.when(inside(*step))
             def _(i=i, src=src, dst=dst, step=step):
                 halo_copy(k, i, src, dst, step).start()
@@ -276,10 +285,10 @@
         weight = lax.rsqrt(smooth_floor + slope0 * slope0 + slope1 * slope1 + slope2 * slope2)
         edge_flux[...] = jnp.where(c == 0, 0.0, slope2 * weight)
 
-    def sweep(k, last):
-        @pl.loop(0, H // CHUNK)
+    def sweep(k, last, base):
+        @pl.loop(0, own // CHUNK)
         def _(step):
-            start = pl.multiple_of(step * CHUNK, 8)
+            start = pl.multiple_of(base + step * CHUNK, 8)
             R = CHUNK
             lane_t = lax.broadcasted_iota(jnp.int32, (R + 8, 128), 1)
             row_t = lax.broadcasted_iota(jnp.int32, (R + 8, W), 0) + (r * H + start - 8)
@@ -357,8 +366,10 @@
                 n += 1
 
     loads[0].wait()
+    send_halos(0, range(10, 10 + 2 * nz))
+    send_halos(0, range(4, 10))
     pack_columns(0)
-    send_halos(0)
+    send_halos(0, range(4))
     loads[1].wait()
 
     def store_gram(i, j, value):
@@ -387,17 +398,6 @@
             anchor[f, rows, :] = video[f, rows, :] + lifted
             target[f, rows, :] = video[f, rows, :] - totals[f] + lifted
 
-    for k in range(PASSES):
-        wait_halos(k)
-        prepare_columns(k)
-        sweep(k, k == PASSES - 1)
-        if k < PASSES - 1:
-            pack_columns(k + 1)
-            send_halos(k + 1)
-
-    out_copy = pltpu.make_async_copy(result, shrunk_hbm, out_sems.at[0])
-    out_copy.start()
-
     def move(d):
         there = lax.rem(z + d, nz)
         rows = pl.ds(pl.multiple_of(there * own, 8), own)
@@ -416,8 +416,25 @@
             device_id=(r, c, source), device_id_type=MESH,
         )
 
-    for d in range(1, nz):
-        move(d).start()
+    for k in range(PASSES):
+        wait_halos(k)
+        prepare_columns(k)
+        if k < PASSES - 1:
+            for b in range(nz):
+                sweep(k, False, b * own)
+                send_halos(k + 1, (10 + 2 * b, 11 + 2 * b))
+            send_halos(k + 1, range(4, 10))
+            pack_columns(k + 1)
+            send_halos(k + 1, range(4))
+        else:
+            for d in range(1, nz + 1):
+                sweep(k, True, lax.rem(z + d, nz) * own)
+                if d < nz:
+                    move(d).start()
+
+    out_copy = pltpu.make_async_copy(result, shrunk_hbm, out_sems.at[0])
+    out_copy.start()
+
     my_rows = pl.ds(pl.multiple_of(z * own, 8), own)
     keep = pltpu.make_async_copy(
         anchor.at[:, my_rows, :], owned.at[pl.ds(z * F, F)], small_sem.at[0]
@@ -591,8 +608,8 @@
             pltpu.SMEM((rank, 128), f32),
             dma((4,)),
             dma((2,)),
-            dma((PASSES, 12)),
-            dma((PASSES, 12)),
+            dma((PASSES, 10 + 2 * nz)),
+            dma((PASSES, 10 + 2 * nz)),
             dma((group,)),
             dma((group,)),
             dma((nz,)),
@@ -614,7 +631,7 @@
     rank = basis.shape[0]
     nz = lax.axis_size("frame")
     fits = (
-        H % nz == 0 and (H // nz) % 8 == 0 and H % CHUNK == 0 and W % 128 == 0
+        H % nz == 0 and (H // nz) % 8 == 0 and (H // nz) % CHUNK == 0 and W % 128 == 0
         and F <= 8 and rank % 8 == 0 and 2 * rank + F * nz <= 128
     )
     run = whole_kernel if fits else local

time: 88.4 us -> 80.2 us (0.907)
  Pallas kernels: 82.6 us -> 74.4 us
    pallas_call x1, Pallas kernels: 82.6 us -> 74.4 us  [whole_kernel(): pl.pallas_call(functools.partial(kernel, (F, H, W, rank, nr, nc, nz)), ou...]
where the time goes in v2:
time: 80.2 us; the launch traced here: 79.9 us
  Pallas kernels  74.4 us (93%)
  local copies, waits for them, and re-layouts  4.9 us (6%)
    pallas_call x1, Pallas kernels, whole_kernel(): pl.pallas_call(functools.partial(kernel, (F, H, W, rank, nr, nc, nz)), ou...  74.4 us
    unnamed x5, local copies, waits for them, and re-layouts  4.13 us

profile of v2, /device:TPU:0, one launch (start us, length us, event | category | flops | bytes accessed | tf_op | source)
XLA Modules:
  0.0 79.9 jit_solution(1259226077281428121)
XLA Ops:
  0.6 74.4 %shard_map.76 = (f32[4,288,256]{2,1,0:T(8,128)}, f32[16,128]{1,0:T(8,128)}, f32[16,72,256]{2,1,0:T(8,128)}) custom-call(f32[4,16]{1,0:T(4,128)} %coeff_ref.1, f32[4,288,256]{2,1,0:T(8,128)} %video_hbm.1, f32[4,288,256]{2,1,0:T(8,128)} %mult_hbm.1, f32[4,288,256]{2,1,0:T(8,128)} %fore_hbm.1, f32[16,288,256]{2,1,0:T(8,128)} %basis_hbm.1), custom_call_target="tpu_custom_call" | custom-call | tf_op jit(solution)/shard_map/pallas_call | solution.py:574
  75.0 0.8 slice_bitcast_fusion
  75.8 0.7 copy.8
  76.4 0.0 copy-start
  76.5 2.5 %copy.11 = f32[4,288,256]{2,1,0:T(8,128)} copy(f32[4,288,256]{2,1,0:T(8,128)} %get-tuple-element.15) | data formatting | bytes 2359296
  78.9 0.0 copy-done
  78.9 1.0 %copy.12 = f32[16,72,256]{2,1,0:T(8,128)} copy(f32[16,72,256]{2,1,0:T(8,128)S(1)} %copy-done) | data formatting | bytes 2359296
Async XLA Ops:
  76.4 2.5 %copy-start = (f32[16,72,256]{2,1,0:T(8,128)S(1)}, f32[16,72,256]{2,1,0:T(8,128)}, u32[]{:S(2)}) copy-start(f32[16,72,256]{2,1,0:T(8,128)} %get-tuple-element.17) | copy-start | bytes 3538948
